TPU v7x, 512 devices: a whole 4x8x8 slice. The times are simulated.
512 devices in a mesh: ctx: 128 (over y, z, core), head: 4 (over x).
Axes of the slice: x: 4, y: 8, z: 8, core: 2. Of those that a mesh axis runs over, the one named last changes fastest.
Arguments:
- tokens: bfloat16 [2, 16384, 4096], P(None, 'ctx', 'head'), may hold values from -6 to 6
- w_query: bfloat16 [4096, 2048], P('ctx', 'head'), may hold values from -0.09375 to 0.09375
- w_key: bfloat16 [4096, 2048], P('ctx', 'head'), may hold values from -0.09375 to 0.09375
- w_value: bfloat16 [4096, 2048], P('ctx', 'head'), may hold values from -0.09375 to 0.09375
- norm_gain: float32 [2048], P('head'), may hold values from 0.1 to 1.9
Outputs:
- attended: bfloat16 [2, 16384, 2048], P(None, 'ctx', 'head')
All inputs are finite; a program needn't handle non-finite values.
Results may differ from a plain program's by a relative error of at most 0.0072.
Values may be sent and summed in bfloat16 or wider, within the bound.
No kernel may reach another device: no remote copies, remote signals or barrier semaphores. Data moves between devices by JAX's collectives and lax.ppermute only.
A program may use at most 192 MiB of HBM per device.

v0:
```python
import jax
import jax.numpy as jnp
from jax import lax
from jax.experimental import pallas as pl
from jax.experimental.pallas import tpu as pltpu
from jax.sharding import PartitionSpec as P


HD = 128
SIDE = 8
CORES = 2


def index(y, z, core):
    return ((y % SIDE) * SIDE + z % SIDE) * CORES + core


def everyone():
    return [(y, z, core) for y in range(SIDE) for z in range(SIDE) for core in range(CORES)]


def across():
    return [(index(y, z, core), index(y, z, 1 - core)) for y, z, core in everyone()]


def along_second(hop):
    return [
        (index(y, z, core), index(y + hop, z, core) if core == 0 else index(y, z + hop, core))
        for y, z, core in everyone()
    ]


def first_groups():
    groups = [[index(y, z, 0) for z in range(SIDE)] for y in range(SIDE)]
    return groups + [[index(y, z, 1) for y in range(SIDE)] for z in range(SIDE)]


def chip_groups():
    return [[index(y, z, core) for y in range(SIDE) for z in range(SIDE)] for core in range(CORES)]


def block_at(number, second):
    far = (number + 1) // 2
    return jnp.where(number % 2 == 1, second + SIDE - far, second + far) % SIDE


def left_of(info_ref, lhs, number, steps):
    core, second, head_at = info_ref[0], info_ref[1], info_ref[2]
    heads = lhs.shape[0]
    at = block_at(number, second)
    parts = []
    for p in range(steps):
        part = jnp.where(core == 0, at // 2, p)
        hop = (head_at + heads - part) % heads
        lane = jnp.where(core == 0, (at % 2) * steps + p, at)
        parts.append(lhs[hop, :, pl.ds(pl.multiple_of(lane * HD, HD), HD)])
    return parts


def early_kernel(heads, count, info_ref, *refs):
    pieces, blocks = refs[:heads], refs[heads : heads + count]
    total, last, lhs, rhs, lhs_sems, rhs_sems = refs[heads + count :]
    depth, columns = rhs.shape[1:]
    steps, group = depth // HD, 2 * HD
    lhs_copies = [pltpu.make_async_copy(r, lhs.at[i], lhs_sems.at[i]) for i, r in enumerate(pieces)]
    rhs_copies = [pltpu.make_async_copy(r, rhs.at[i], rhs_sems.at[i]) for i, r in enumerate(blocks)]
    for copy in lhs_copies + rhs_copies:
        copy.start()
    for copy in lhs_copies:
        copy.wait()
    for number in range(count, count + last.shape[1] // depth):
        cols = slice((number - count) * depth, (number - count + 1) * depth)
        last[:, cols] = jnp.concatenate(left_of(info_ref, lhs, number, steps), axis=1)
    rhs_copies[0].wait()
    left = jnp.concatenate(left_of(info_ref, lhs, 0, steps), axis=1)
    for g in range(columns // group):
        cols = slice(g * group, (g + 1) * group)
        total[:, cols] = jnp.dot(left, rhs[0, :, cols], preferred_element_type=jnp.float32)

    def two(pair, _):
        number = 2 * pair + 1
        for i in range(2):
            pltpu.make_async_copy(blocks[0], rhs.at[number + i], rhs_sems.at[number + i]).wait()
        left = [part for i in range(2) for part in left_of(info_ref, lhs, number + i, steps)]
        left = jnp.concatenate(left, axis=1)
        for g in range(columns // group):
            cols = slice(g * group, (g + 1) * group)
            right = rhs[pl.ds(number, 2), :, cols].reshape(2 * depth, group)
            total[:, cols] += jnp.dot(left, right, preferred_element_type=jnp.float32)
        return 0

    lax.fori_loop(0, count // 2, two, 0)


def late_kernel(seqs, *refs):
    count = len(refs) - 6
    blocks, (left, sums, qkv, states, rhs, sems) = refs[:count], refs[count:]
    columns = sums.shape[1]
    half, group = columns // 3, 2 * HD
    copies, ends, end = [], [], 0
    for i, block in enumerate(blocks):
        rows = pl.ds(end, block.shape[0])
        copies.append(pltpu.make_async_copy(block, rhs.at[rows], sems.at[i]))
        end += block.shape[0]
        ends.append(end)
    for copy in copies:
        copy.start()
    copies[0].wait()
    first = ends[0]
    for g in range(columns // group):
        cols = slice(g * group, (g + 1) * group)
        sums[:, cols] += jnp.dot(left[:, :first], rhs[:first, cols], preferred_element_type=jnp.float32)
    for copy in copies[1:]:
        copy.wait()
    for g in range(columns // group):
        cols = slice(g * group, (g + 1) * group)
        total = sums[:, cols] + jnp.dot(left[:, first:], rhs[first:, cols], preferred_element_type=jnp.float32)
        if g * group < 2 * half:
            total = total / (1.0 + jnp.exp(-total))
        qkv[:, cols] = total.astype(qkv.dtype)
    span = sums.shape[0] // (CORES * seqs)
    for s in range(seqs):
        for h in range(half // HD):
            acc = jnp.zeros((HD, HD), jnp.float32)
            for c in range(CORES):
                at = pl.ds((c * seqs + s) * span, span)
                key = qkv[at, pl.ds(half + h * HD, HD)]
                value = qkv[at, pl.ds(2 * half + h * HD, HD)]
                acc += lax.dot_general(key, value, (((0,), (0,)), ((), ())), preferred_element_type=jnp.float32)
            states[s, h] = acc


def call_info(core, second, head_at):
    return jnp.stack([core, second, head_at]).astype(jnp.int32)


SMEM = pl.BlockSpec(memory_space=pltpu.SMEM)
ANY = pl.BlockSpec(memory_space=pl.ANY)
VMEM = pl.BlockSpec(memory_space=pltpu.VMEM)


def early_product(info, pieces, blocks, later):
    rows, (depth, columns) = pieces[0].shape[0], blocks[0].shape
    heads, count = len(pieces), len(blocks)

    def kernel(*refs):
        early_kernel(heads, count, *refs)

    return pl.pallas_call(
        kernel,
        out_shape=(
            jax.ShapeDtypeStruct((rows, columns), jnp.float32),
            jax.ShapeDtypeStruct((rows, later * depth), pieces[0].dtype),
        ),
        in_specs=[SMEM] + [ANY] * (heads + count),
        out_specs=(VMEM, VMEM),
        scratch_shapes=[
            pltpu.VMEM((heads,) + pieces[0].shape, pieces[0].dtype),
            pltpu.VMEM((count, depth, columns), blocks[0].dtype),
            pltpu.SemaphoreType.DMA((heads,)),
            pltpu.SemaphoreType.DMA((count,)),
        ],
        cost_estimate=pl.CostEstimate(
            flops=2 * rows * columns * depth * count, bytes_accessed=8 << 20, transcendentals=0
        ),
    )(info, *pieces, *blocks)


def late_product(blocks, left, sums, seqs):
    rows, columns = sums.shape

    def kernel(*refs):
        count = len(blocks)
        sums_ref, total = refs[count + 1], refs[-1]
        total[...] = sums_ref[...]
        late_kernel(seqs, *refs[: count + 1], total, *refs[count + 2 : -1])

    return pl.pallas_call(
        kernel,
        out_shape=(
            jax.ShapeDtypeStruct((rows, columns), jnp.bfloat16),
            jax.ShapeDtypeStruct((seqs, columns // 3 // HD, HD, HD), jnp.float32),
        ),
        in_specs=[ANY] * len(blocks) + [VMEM] * 2,
        out_specs=(VMEM, VMEM),
        scratch_shapes=[
            pltpu.VMEM((left.shape[1], columns), left.dtype),
            pltpu.SemaphoreType.DMA((len(blocks),)),
            pltpu.VMEM((rows, columns), jnp.float32),
        ],
    )(*blocks, left, sums)


def scan_kernel(slices_ref, prefix_ref):
    def one(block, carried):
        prefix_ref[block] = carried.astype(prefix_ref.dtype)
        return carried + slices_ref[block]

    lax.fori_loop(0, slices_ref.shape[0], one, jnp.zeros(slices_ref.shape[1:], jnp.float32), unroll=8)


def exclusive(slices):
    return pl.pallas_call(
        scan_kernel,
        out_shape=jax.ShapeDtypeStruct(slices.shape, jnp.bfloat16),
        in_specs=[VMEM],
        out_specs=VMEM,
    )(slices)


def both_spans(qkv, seqs, s, h, kind):
    half = qkv.shape[1] // 3
    span = qkv.shape[0] // (CORES * seqs)
    lanes = pl.ds(kind * half + h * HD, HD)
    return jnp.concatenate([qkv[pl.ds((c * seqs + s) * span, span), lanes] for c in range(CORES)], axis=0)


def local_kernel(seqs, qkv, out):
    both = qkv.shape[0] // seqs
    ahead = lax.broadcasted_iota(jnp.int32, (both, both), 0)
    causal = ahead >= lax.broadcasted_iota(jnp.int32, (both, both), 1)
    for s in range(seqs):
        for h in range(out.shape[1]):
            query, key, value = (both_spans(qkv, seqs, s, h, kind) for kind in range(3))
            scores = lax.dot_general(query, key, (((1,), (1,)), ((), ())), preferred_element_type=jnp.float32)
            masked = jnp.where(causal, scores, 0.0).astype(jnp.bfloat16)
            out[s, h] = jnp.dot(masked, value, preferred_element_type=jnp.float32)


def local_part(qkv, seqs):
    rows, columns = qkv.shape

    def kernel(*refs):
        local_kernel(seqs, *refs)

    return pl.pallas_call(
        kernel,
        out_shape=jax.ShapeDtypeStruct((seqs, columns // 3 // HD, rows // seqs, HD), jnp.float32),
        in_specs=[VMEM],
        out_specs=VMEM,
    )(qkv)


def attend_kernel(seqs, info_ref, qkv, local, prefix, gain, whole, other, spans):
    span = qkv.shape[0] // (CORES * seqs)
    for s in range(seqs):
        for h in range(local.shape[1]):
            query = both_spans(qkv, seqs, s, h, 0)
            total = local[s, h] + jnp.dot(query, prefix[s, h], preferred_element_type=jnp.float32)
            scale_inv = lax.rsqrt(jnp.mean(total * total, axis=-1, keepdims=True) + 1e-06)
            normed = (total * scale_inv * gain[:, pl.ds(h * HD, HD)]).astype(whole.dtype)
            for c in range(CORES):
                spans[c, s, :, pl.ds(h * HD, HD)] = normed[c * span : (c + 1) * span]
    core, half = info_ref[0], other.shape[-1]
    whole[:, :, pl.ds(pl.multiple_of(core * half, HD), half)] = spans[core]
    other[...] = spans[1 - core]


def attend(info, qkv, local, prefix, gain, seqs):
    rows, columns = qkv.shape
    shape = (seqs, rows // CORES // seqs, columns // 3)

    def kernel(*refs):
        attend_kernel(seqs, *refs)

    return pl.pallas_call(
        kernel,
        out_shape=(
            jax.ShapeDtypeStruct(shape[:-1] + (CORES * shape[-1],), jnp.bfloat16),
            jax.ShapeDtypeStruct(shape, jnp.bfloat16),
        ),
        in_specs=[SMEM] + [VMEM] * 4,
        out_specs=(VMEM, VMEM),
        scratch_shapes=[pltpu.VMEM((CORES,) + shape, jnp.bfloat16)],
    )(info, qkv, local, prefix, gain)


def body(tokens, w_query, w_key, w_value, norm_gain, *, heads):
    seq_count, span_len, shard = tokens.shape
    features = w_query.shape[1]
    half = features // CORES
    rows = seq_count * span_len
    ctx_at = lax.axis_index("ctx")
    core = ctx_at % CORES
    z_at = (ctx_at // CORES) % SIDE
    y_at = ctx_at // (CORES * SIDE)
    second = jnp.where(core == 0, y_at, z_at)
    head_at = lax.axis_index("head")
    is_first = core == 0

    def pair(own, came):
        return jnp.concatenate([jnp.where(is_first, own, came), jnp.where(is_first, came, own)], axis=0)

    low = jnp.concatenate([w[:, :half] for w in (w_query, w_key, w_value)], axis=1)
    high = jnp.concatenate([w[:, half:] for w in (w_query, w_key, w_value)], axis=1)
    halves = [jnp.where(is_first, w[:, :half], w[:, half:]) for w in (w_query, w_key, w_value)]
    kept = jnp.concatenate(halves, axis=1)
    came = lax.ppermute(jnp.where(is_first, high, low), "ctx", across())
    chip_rows = pair(kept, came)

    natural = tokens.reshape(rows, shard)
    per_y = shard // 2
    turned = natural.reshape(rows, 2, SIDE, per_y // SIDE).transpose(0, 2, 1, 3).reshape(rows, shard)
    came = lax.ppermute(jnp.where(is_first, turned, natural), "ctx", across())
    chip_tokens = pair(jnp.where(is_first, natural, turned), came)
    pieces = [chip_tokens]
    for hop in range(1, heads):
        ring = [(i, (i + hop) % heads) for i in range(heads)]
        pieces.append(lax.ppermute(chip_tokens, "head", ring))

    depth, columns = chip_rows.shape
    copies = jnp.broadcast_to(chip_rows[None], (SIDE, depth, columns))
    block = lax.all_to_all(copies, "ctx", 0, 0, tiled=True, axis_index_groups=first_groups())
    block = block.reshape(SIDE * depth, columns)

    blocks = [block]
    up = down = block
    for _ in range(1, SIDE // 2 - 1):
        up = lax.ppermute(up, "ctx", along_second(1))
        down = lax.ppermute(down, "ctx", along_second(-1))
        blocks += [up, down]
    far_up = lax.ppermute(up, "ctx", along_second(1))
    far_down = lax.ppermute(down, "ctx", along_second(-1))
    deep = block.shape[0] // 2
    top = lax.ppermute(up[:deep], "ctx", along_second(2))
    bottom = lax.ppermute(down[deep:], "ctx", along_second(-2))
    info = call_info(core, second, head_at)
    sums, left = early_product(info, pieces, blocks, SIDE - len(blocks))
    qkv, states = late_product([far_up, far_down, top, bottom], left, sums, seq_count)

    chips = SIDE * SIDE
    slices = lax.all_to_all(
        states.reshape(chips, -1, HD), "ctx", 0, 0, tiled=True, axis_index_groups=chip_groups()
    )
    local = local_part(qkv, seq_count)
    prefix = lax.all_to_all(exclusive(slices), "ctx", 0, 0, tiled=True, axis_index_groups=chip_groups())
    gain = jnp.where(is_first, norm_gain[:half], norm_gain[half:]).reshape(1, half)
    whole, other = attend(info, qkv, local, prefix.reshape(states.shape), gain, seq_count)
    came = lax.ppermute(other, "ctx", across())
    return lax.dynamic_update_slice(whole, came, (0, 0, (1 - core) * half))


def solution(mesh):
    sizes = dict(mesh.shape)
    in_specs = (P(None, "ctx", "head"), P("ctx", "head"), P("ctx", "head"), P("ctx", "head"), P("head"))

    def step(*operands):
        return body(*operands, heads=sizes["head"])

    return jax.shard_map(step, mesh=mesh, in_specs=in_specs, out_specs=P(None, "ctx", "head"), check_vma=False)
```

profile of v0, /device:TPU:1, one launch (start us, length us, event | category | flops | bytes accessed | tf_op | source)
XLA Modules:
  0.0 175.7 jit_solution(13654243540481532510)
XLA Ops:
  1.6 8.7 %collective-permute-start = (bf16[32,768]{1,0:T(8,128)(2,1)S(1)}, bf16[32,768]{1,0:T(8,128)(2,1)S(1)}, u32[]{:S(2)}, u32[]{:S(2)}) collective-permute-start(bf16[32,768]{1,0:T(8,128)(2,1)S(1)} %maximum_select_fusion), channel_id=1, source_target_pairs={{0,4},{4,0},{8,12},{12,8},{16,20},{20,16},{24,28},{28,24},{32,36},... | collective-permute-start | bytes 147464 | tf_op jit(solution)/shard_map/ppermute | solution.py:298
  11.2 0.9 broadcast_in_dim.2
  12.2 3.5 %all-to-all-start = ((bf16[8,64,768]{2,1,0:T(8,128)(2,1)}), bf16[8,64,768]{2,1,0:T(8,128)(2,1)S(1)}, u32[]{:S(2)}, u32[]{:S(2)}) async-start(bf16[8,64,768]{2,1,0:T(8,128)(2,1)} %broadcast_in_dim.2), calls=%async_computation | async-start | bytes 1572864 | tf_op jit(solution)/shard_map/all_to_all | solution.py:313
  16.9 3.7 %collective-permute-start.9 = (bf16[256,1024]{1,0:T(8,128)(2,1)S(1)}, bf16[256,1024]{1,0:T(8,128)(2,1)S(1)}, u32[]{:S(2)}, u32[]{:S(2)}) collective-permute-start(bf16[256,1024]{1,0:T(8,128)(2,1)S(1)} %bitcast_select_fusion), channel_id=1, source_target_pairs={{0,4},{4,0},{8,12},{12,8},{16,20},{20,16},{24,28},{28,24},{32,36},... | collective-permute-start | bytes 1572872 | tf_op jit(solution)/shard_map/ppermute | solution.py:304
  20.6 10.1 %all-to-all-done = bf16[8,64,768]{2,1,0:T(8,128)(2,1)S(1)} async-done(((bf16[8,64,768]{2,1,0:T(8,128)(2,1)}), bf16[8,64,768]{2,1,0:T(8,128)(2,1)S(1)}, u32[]{:S(2)}, u32[]{:S(2)}) %all-to-all-start) | async-done | bytes 786464 | tf_op jit(solution)/shard_map/all_to_all | solution.py:313
  30.7 2.3 %collective-permute-start.1 = (bf16[512,768]{1,0:T(8,128)(2,1)S(1)}, bf16[512,768]{1,0:T(8,128)(2,1)S(1)}, u32[]{:S(2)}, u32[]{:S(2)}) collective-permute-start(bf16[512,768]{1,0:T(8,128)(2,1)S(1)} %bitcast.18), channel_id=1, source_target_pairs={{0,64},{4,12},{8,72},{12,20},{16,80},{20,28},{24,88},{28,36},{32,9... | collective-permute-start | bytes 2359304 | tf_op jit(solution)/shard_map/ppermute | solution.py:319
  33.0 8.3 %collective-permute-start.4 = (bf16[512,768]{1,0:T(8,128)(2,1)S(1)}, bf16[512,768]{1,0:T(8,128)(2,1)S(1)}, u32[]{:S(2)}, u32[]{:S(2)}) collective-permute-start(bf16[512,768]{1,0:T(8,128)(2,1)S(1)} %bitcast.19), channel_id=1, source_target_pairs={{0,448},{4,60},{8,456},{12,4},{16,464},{20,12},{24,472},{28,20},{3... | collective-permute-start | bytes 2359304 | tf_op jit(solution)/shard_map/ppermute | solution.py:320
  41.4 7.3 %collective-permute-done.1.refs_6_ = bf16[512,768]{1,0:T(8,128)(2,1)S(1)} collective-permute-done((bf16[512,768]{1,0:T(8,128)(2,1)S(1)}, bf16[512,768]{1,0:T(8,128)(2,1)S(1)}, u32[]{:S(2)}, u32[]{:S(2)}) %collective-permute-start.1) | collective-permute-done | bytes 786464 | tf_op jit(solution)/shard_map/ppermute | solution.py:319
  48.7 1.9 %collective-permute-start.2 = (bf16[512,768]{1,0:T(8,128)(2,1)S(1)}, bf16[512,768]{1,0:T(8,128)(2,1)S(1)}, u32[]{:S(2)}, u32[]{:S(2)}) collective-permute-start(bf16[512,768]{1,0:T(8,128)(2,1)S(1)} %collective-permute-done.1.refs_6_), channel_id=1, source_target_pairs={{0,64},{4,12},{8,72},{12,20},{16,80},{20,28},{24,88},{28,36},{32,9... | collective-permute-start | bytes 2359304 | tf_op jit(solution)/shard_map/ppermute | solution.py:319
  50.6 4.8 %collective-permute-start.5 = (bf16[512,768]{1,0:T(8,128)(2,1)S(1)}, bf16[512,768]{1,0:T(8,128)(2,1)S(1)}, u32[]{:S(2)}, u32[]{:S(2)}) collective-permute-start(bf16[512,768]{1,0:T(8,128)(2,1)S(1)} %collective-permute-done.4.refs_7_), channel_id=1, source_target_pairs={{0,448},{4,60},{8,456},{12,4},{16,464},{20,12},{24,472},{28,20},{3... | collective-permute-start | bytes 2359304 | tf_op jit(solution)/shard_map/ppermute | solution.py:320
  55.6 3.1 %collective-permute-start.10 = (bf16[512,1024]{1,0:T(8,128)(2,1)S(1)}, bf16[512,1024]{1,0:T(8,128)(2,1)S(1)}, u32[]{:S(2)}, u32[]{:S(2)}) collective-permute-start(bf16[512,1024]{1,0:T(8,128)(2,1)S(1)} %pad_maximum_fusion.refs_1_), channel_id=1, source_target_pairs={{0,1},{1,2},{2,3},{3,0},{4,5},{5,6},{6,7},{7,4},{8,9},{9,10},{10,1... | collective-permute-start | bytes 3145736 | tf_op jit(solution)/shard_map/ppermute | solution.py:309
  58.7 4.4 %collective-permute-start.11 = (bf16[512,1024]{1,0:T(8,128)(2,1)S(1)}, bf16[512,1024]{1,0:T(8,128)(2,1)S(1)}, u32[]{:S(2)}, u32[]{:S(2)}) collective-permute-start(bf16[512,1024]{1,0:T(8,128)(2,1)S(1)} %pad_maximum_fusion.refs_1_), channel_id=1, source_target_pairs={{0,2},{1,3},{2,0},{3,1},{4,6},{5,7},{6,4},{7,5},{8,10},{9,11},{10,... | collective-permute-start | bytes 3145736 | tf_op jit(solution)/shard_map/ppermute | solution.py:309
  63.1 3.1 %collective-permute-start.12 = (bf16[512,1024]{1,0:T(8,128)(2,1)S(1)}, bf16[512,1024]{1,0:T(8,128)(2,1)}, u32[]{:S(2)}, u32[]{:S(2)}) collective-permute-start(bf16[512,1024]{1,0:T(8,128)(2,1)S(1)} %pad_maximum_fusion.refs_1_), channel_id=1, source_target_pairs={{0,3},{1,0},{2,1},{3,2},{4,7},{5,4},{6,5},{7,6},{8,11},{9,8},{10,9... | collective-permute-start | bytes 3145736 | tf_op jit(solution)/shard_map/ppermute | solution.py:309
  66.2 1.9 %collective-permute-start.3 = (bf16[512,768]{1,0:T(8,128)(2,1)S(1)}, bf16[512,768]{1,0:T(8,128)(2,1)S(1)}, u32[]{:S(2)}, u32[]{:S(2)}) collective-permute-start(bf16[512,768]{1,0:T(8,128)(2,1)S(1)} %collective-permute-done.2.refs_8_), channel_id=1, source_target_pairs={{0,64},{4,12},{8,72},{12,20},{16,80},{20,28},{24,88},{28,36},{32,9... | collective-permute-start | bytes 2359304 | tf_op jit(solution)/shard_map/ppermute | solution.py:322
  68.1 4.6 %collective-permute-start.6 = (bf16[512,768]{1,0:T(8,128)(2,1)S(1)}, bf16[512,768]{1,0:T(8,128)(2,1)}, u32[]{:S(2)}, u32[]{:S(2)}) collective-permute-start(bf16[512,768]{1,0:T(8,128)(2,1)S(1)} %collective-permute-done.5.refs_9_), channel_id=1, source_target_pairs={{0,448},{4,60},{8,456},{12,4},{16,464},{20,12},{24,472},{28,20},{3... | collective-permute-start | bytes 2359304 | tf_op jit(solution)/shard_map/ppermute | solution.py:323
  74.3 8.6 %collective-permute-done.10.refs_2_ = bf16[512,1024]{1,0:T(8,128)(2,1)S(1)} collective-permute-done((bf16[512,1024]{1,0:T(8,128)(2,1)S(1)}, bf16[512,1024]{1,0:T(8,128)(2,1)S(1)}, u32[]{:S(2)}, u32[]{:S(2)}) %collective-permute-start.10) | collective-permute-done | bytes 1048608 | tf_op jit(solution)/shard_map/ppermute | solution.py:309
  82.8 1.9 %collective-permute-start.7 = (bf16[256,768]{1,0:T(8,128)(2,1)}, bf16[256,768]{1,0:T(8,128)(2,1)}, u32[]{:S(2)}, u32[]{:S(2)}) collective-permute-start(bf16[256,768]{1,0:T(8,128)(2,1)} %slice.46), channel_id=1, source_target_pairs={{0,128},{4,20},{8,136},{12,28},{16,144},{20,36},{24,152},{28,44},{... | collective-permute-start | bytes 1179656 | tf_op jit(solution)/shard_map/ppermute | solution.py:325
  84.8 21.5 %collective-permute-done.11.refs_3_ = bf16[512,1024]{1,0:T(8,128)(2,1)S(1)} collective-permute-done((bf16[512,1024]{1,0:T(8,128)(2,1)S(1)}, bf16[512,1024]{1,0:T(8,128)(2,1)S(1)}, u32[]{:S(2)}, u32[]{:S(2)}) %collective-permute-start.11) | collective-permute-done | bytes 1048608 | tf_op jit(solution)/shard_map/ppermute | solution.py:309
  106.3 1.0 copy-done.6
  107.3 2.5 %collective-permute-start.8 = (bf16[256,768]{1,0:T(8,128)(2,1)}, bf16[256,768]{1,0:T(8,128)(2,1)}, u32[]{:S(2)}, u32[]{:S(2)}) collective-permute-start(bf16[256,768]{1,0:T(8,128)(2,1)} %slice.47), channel_id=1, source_target_pairs={{0,384},{4,52},{8,392},{12,60},{16,400},{20,4},{24,408},{28,12},{3... | collective-permute-start | bytes 1179656 | tf_op jit(solution)/shard_map/ppermute | solution.py:326
  110.5 8.1 %shard_map.55 = (f32[512,768]{1,0:T(8,128)}, bf16[512,1536]{1,0:T(8,128)(2,1)}) custom-call(s32[3]{0:T(128)} %pad_add_fusion.refs_0_, bf16[512,1024]{1,0:T(8,128)(2,1)} %copy-done.1, bf16[512,1024]{1,0:T(8,128)(2,1)} %copy-done.5, bf16[512,1024]{1,0:T(8,128)(2,1)} %copy-done.6, bf16[512,1024]{1,0:T(8,128)(2,1)} %collective-permute-done.12.refs_4_, ...), custom_call_target="tpu_custom_call" | custom-call | flops 2013265920 | bytes 8388608 | tf_op jit(solution)/shard_map/pallas_call | solution.py:149
  118.6 1.6 collective-permute-done.8.refs_3_
  120.2 0.9 copy-done.9
  121.0 6.1 %shard_map.56 = (bf16[512,768]{1,0:T(8,128)(2,1)}, f32[2,2,128,128]{3,2,1,0:T(8,128)}) custom-call(bf16[512,768]{1,0:T(8,128)(2,1)} %copy-done.9, bf16[512,768]{1,0:T(8,128)(2,1)} %collective-permute-done.6.refs_1_, bf16[256,768]{1,0:T(8,128)(2,1)} %collective-permute-done.7.refs_2_, bf16[256,768]{1,0:T(8,128)(2,1)} %collective-permute-done.8.refs_3_, ...), custom_call_target="tpu_custom_call" | custom-call | tf_op jit(solution)/shard_map/pallas_call | solution.py:178
  127.1 17.9 %all_to_all.15.slices_ref = f32[64,8,128]{2,1,0:T(8,128)} all-to-all(f32[64,8,128]{2,1,0:T(8,128)} %bitcast.24), channel_id=1, replica_groups={{0,8,16,24,32,40,48,56,64,72,80,88,96,104,112,120,128,136,144,152,160,1..., dimensions={0} | all-to-all | bytes 524288 | tf_op jit(solution)/shard_map/all_to_all | solution.py:332
  145.1 1.7 shard_map.58
  146.7 4.6 %all-to-all-start.2 = ((bf16[64,8,128]{2,1,0:T(8,128)(2,1)}), bf16[64,8,128]{2,1,0:T(8,128)(2,1)S(1)}, u32[]{:S(2)}, u32[]{:S(2)}) async-start(bf16[64,8,128]{2,1,0:T(8,128)(2,1)} %shard_map.58), calls=%async_computation.2 | async-start | bytes 262144 | tf_op jit(solution)/shard_map/all_to_all | solution.py:336
  152.0 2.6 %shard_map.57.refs_2_ = f32[2,2,256,128]{3,2,1,0:T(8,128)} custom-call(bf16[512,768]{1,0:T(8,128)(2,1)} %get-tuple-element.13.refs_0_.refs_1_), custom_call_target="tpu_custom_call" | custom-call | tf_op jit(solution)/shard_map/pallas_call | solution.py:236
  154.6 8.4 %all-to-all-done.2 = bf16[64,8,128]{2,1,0:T(8,128)(2,1)S(1)} async-done(((bf16[64,8,128]{2,1,0:T(8,128)(2,1)}), bf16[64,8,128]{2,1,0:T(8,128)(2,1)S(1)}, u32[]{:S(2)}, u32[]{:S(2)}) %all-to-all-start.2) | async-done | bytes 131104 | tf_op jit(solution)/shard_map/all_to_all | solution.py:336
  163.6 2.4 %shard_map.59 = (bf16[2,128,512]{2,1,0:T(8,128)(2,1)}, bf16[2,128,256]{2,1,0:T(8,128)(2,1)}) custom-call(s32[3]{0:T(128)} %pad_add_fusion.refs_0_, bf16[512,768]{1,0:T(8,128)(2,1)} %get-tuple-element.13.refs_0_.refs_1_, f32[2,2,256,128]{3,2,1,0:T(8,128)} %shard_map.57.refs_2_, bf16[2,2,128,128]{3,2,1,0:T(8,128)(2,1)} %bitcast.23, f32[1,256]{1,0:T(1,128)} %bitcast.25), custom_call_target="tpu_custom_call" | custom-call | tf_op jit(solution)/shard_map/pallas_call | solution.py:266
  166.1 7.8 %collective-permute-start.13 = (bf16[2,128,256]{2,1,0:T(8,128)(2,1)}, bf16[2,128,256]{2,1,0:T(8,128)(2,1)S(1)}, u32[]{:S(2)}, u32[]{:S(2)}) collective-permute-start(bf16[2,128,256]{2,1,0:T(8,128)(2,1)} %get-tuple-element.16), channel_id=1, source_target_pairs={{0,4},{4,0},{8,12},{12,8},{16,20},{20,16},{24,28},{28,24},{32,36},... | collective-permute-start | bytes 393224 | tf_op jit(solution)/shard_map/ppermute | solution.py:339
  173.9 1.2 collective-permute-done.13
  (48 shorter events, 7.9 us)
Async XLA Ops:
  0.7 15.0 %copy-start = (bf16[2,128,1024]{2,1,0:T(8,128)(2,1)S(1)}, bf16[2,128,1024]{2,1,0:T(8,128)(2,1)}, u32[]{:S(2)}) copy-start(bf16[2,128,1024]{2,1,0:T(8,128)(2,1)} %param.5) | copy-start | bytes 1572868
  1.6 9.6 %collective-permute-start = (bf16[32,768]{1,0:T(8,128)(2,1)S(1)}, bf16[32,768]{1,0:T(8,128)(2,1)S(1)}, u32[]{:S(2)}, u32[]{:S(2)}) collective-permute-start(bf16[32,768]{1,0:T(8,128)(2,1)S(1)} %maximum_select_fusion), channel_id=1, source_target_pairs={{0,4},{4,0},{8,12},{12,8},{16,20},{20,16},{24,28},{28,24},{32,36},... | collective-permute-start | bytes 147464 | tf_op jit(solution)/shard_map/ppermute | solution.py:298
  12.2 18.5 %all-to-all-start = ((bf16[8,64,768]{2,1,0:T(8,128)(2,1)}), bf16[8,64,768]{2,1,0:T(8,128)(2,1)S(1)}, u32[]{:S(2)}, u32[]{:S(2)}) async-start(bf16[8,64,768]{2,1,0:T(8,128)(2,1)} %broadcast_in_dim.2), calls=%async_computation | async-start | bytes 1572864 | tf_op jit(solution)/shard_map/all_to_all | solution.py:313
  16.9 24.4 %collective-permute-start.9 = (bf16[256,1024]{1,0:T(8,128)(2,1)S(1)}, bf16[256,1024]{1,0:T(8,128)(2,1)S(1)}, u32[]{:S(2)}, u32[]{:S(2)}) collective-permute-start(bf16[256,1024]{1,0:T(8,128)(2,1)S(1)} %bitcast_select_fusion), channel_id=1, source_target_pairs={{0,4},{4,0},{8,12},{12,8},{16,20},{20,16},{24,28},{28,24},{32,36},... | collective-permute-start | bytes 1572872 | tf_op jit(solution)/shard_map/ppermute | solution.py:304
  30.7 24.9 %copy-start.2 = (bf16[8,64,768]{2,1,0:T(8,128)(2,1)}, bf16[8,64,768]{2,1,0:T(8,128)(2,1)S(1)}, u32[]{:S(2)}) copy-start(bf16[8,64,768]{2,1,0:T(8,128)(2,1)S(1)} %all-to-all-done) | copy-start | bytes 2359300
  30.7 18.0 %collective-permute-start.1 = (bf16[512,768]{1,0:T(8,128)(2,1)S(1)}, bf16[512,768]{1,0:T(8,128)(2,1)S(1)}, u32[]{:S(2)}, u32[]{:S(2)}) collective-permute-start(bf16[512,768]{1,0:T(8,128)(2,1)S(1)} %bitcast.18), channel_id=1, source_target_pairs={{0,64},{4,12},{8,72},{12,20},{16,80},{20,28},{24,88},{28,36},{32,9... | collective-permute-start | bytes 2359304 | tf_op jit(solution)/shard_map/ppermute | solution.py:319
  33.0 17.7 %collective-permute-start.4 = (bf16[512,768]{1,0:T(8,128)(2,1)S(1)}, bf16[512,768]{1,0:T(8,128)(2,1)S(1)}, u32[]{:S(2)}, u32[]{:S(2)}) collective-permute-start(bf16[512,768]{1,0:T(8,128)(2,1)S(1)} %bitcast.19), channel_id=1, source_target_pairs={{0,448},{4,60},{8,456},{12,4},{16,464},{20,12},{24,472},{28,20},{3... | collective-permute-start | bytes 2359304 | tf_op jit(solution)/shard_map/ppermute | solution.py:320
  48.7 25.6 %copy-start.7 = (bf16[512,768]{1,0:T(8,128)(2,1)}, bf16[512,768]{1,0:T(8,128)(2,1)S(1)}, u32[]{:S(2)}) copy-start(bf16[512,768]{1,0:T(8,128)(2,1)S(1)} %collective-permute-done.1.refs_6_) | copy-start | bytes 2359300
  48.7 17.5 %collective-permute-start.2 = (bf16[512,768]{1,0:T(8,128)(2,1)S(1)}, bf16[512,768]{1,0:T(8,128)(2,1)S(1)}, u32[]{:S(2)}, u32[]{:S(2)}) collective-permute-start(bf16[512,768]{1,0:T(8,128)(2,1)S(1)} %collective-permute-done.1.refs_6_), channel_id=1, source_target_pairs={{0,64},{4,12},{8,72},{12,20},{16,80},{20,28},{24,88},{28,36},{32,9... | collective-permute-start | bytes 2359304 | tf_op jit(solution)/shard_map/ppermute | solution.py:319
  50.6 23.6 %copy-start.8 = (bf16[512,768]{1,0:T(8,128)(2,1)}, bf16[512,768]{1,0:T(8,128)(2,1)S(1)}, u32[]{:S(2)}) copy-start(bf16[512,768]{1,0:T(8,128)(2,1)S(1)} %collective-permute-done.4.refs_7_) | copy-start | bytes 2359300
  50.6 17.5 %collective-permute-start.5 = (bf16[512,768]{1,0:T(8,128)(2,1)S(1)}, bf16[512,768]{1,0:T(8,128)(2,1)S(1)}, u32[]{:S(2)}, u32[]{:S(2)}) collective-permute-start(bf16[512,768]{1,0:T(8,128)(2,1)S(1)} %collective-permute-done.4.refs_7_), channel_id=1, source_target_pairs={{0,448},{4,60},{8,456},{12,4},{16,464},{20,12},{24,472},{28,20},{3... | collective-permute-start | bytes 2359304 | tf_op jit(solution)/shard_map/ppermute | solution.py:320
  55.6 54.9 %copy-start.1 = (bf16[512,1024]{1,0:T(8,128)(2,1)}, bf16[512,1024]{1,0:T(8,128)(2,1)S(1)}, u32[]{:S(2)}) copy-start(bf16[512,1024]{1,0:T(8,128)(2,1)S(1)} %pad_maximum_fusion.refs_1_) | copy-start | bytes 3145732
  55.6 27.2 %collective-permute-start.10 = (bf16[512,1024]{1,0:T(8,128)(2,1)S(1)}, bf16[512,1024]{1,0:T(8,128)(2,1)S(1)}, u32[]{:S(2)}, u32[]{:S(2)}) collective-permute-start(bf16[512,1024]{1,0:T(8,128)(2,1)S(1)} %pad_maximum_fusion.refs_1_), channel_id=1, source_target_pairs={{0,1},{1,2},{2,3},{3,0},{4,5},{5,6},{6,7},{7,4},{8,9},{9,10},{10,1... | collective-permute-start | bytes 3145736 | tf_op jit(solution)/shard_map/ppermute | solution.py:309
  58.7 47.6 %collective-permute-start.11 = (bf16[512,1024]{1,0:T(8,128)(2,1)S(1)}, bf16[512,1024]{1,0:T(8,128)(2,1)S(1)}, u32[]{:S(2)}, u32[]{:S(2)}) collective-permute-start(bf16[512,1024]{1,0:T(8,128)(2,1)S(1)} %pad_maximum_fusion.refs_1_), channel_id=1, source_target_pairs={{0,2},{1,3},{2,0},{3,1},{4,6},{5,7},{6,4},{7,5},{8,10},{9,11},{10,... | collective-permute-start | bytes 3145736 | tf_op jit(solution)/shard_map/ppermute | solution.py:309
  63.1 47.4 %collective-permute-start.12 = (bf16[512,1024]{1,0:T(8,128)(2,1)S(1)}, bf16[512,1024]{1,0:T(8,128)(2,1)}, u32[]{:S(2)}, u32[]{:S(2)}) collective-permute-start(bf16[512,1024]{1,0:T(8,128)(2,1)S(1)} %pad_maximum_fusion.refs_1_), channel_id=1, source_target_pairs={{0,3},{1,0},{2,1},{3,2},{4,7},{5,4},{6,5},{7,6},{8,11},{9,8},{10,9... | collective-permute-start | bytes 3145736 | tf_op jit(solution)/shard_map/ppermute | solution.py:309
  66.2 44.3 %copy-start.3 = (bf16[512,768]{1,0:T(8,128)(2,1)}, bf16[512,768]{1,0:T(8,128)(2,1)S(1)}, u32[]{:S(2)}) copy-start(bf16[512,768]{1,0:T(8,128)(2,1)S(1)} %collective-permute-done.2.refs_8_) | copy-start | bytes 2359300
  66.2 54.0 %collective-permute-start.3 = (bf16[512,768]{1,0:T(8,128)(2,1)S(1)}, bf16[512,768]{1,0:T(8,128)(2,1)S(1)}, u32[]{:S(2)}, u32[]{:S(2)}) collective-permute-start(bf16[512,768]{1,0:T(8,128)(2,1)S(1)} %collective-permute-done.2.refs_8_), channel_id=1, source_target_pairs={{0,64},{4,12},{8,72},{12,20},{16,80},{20,28},{24,88},{28,36},{32,9... | collective-permute-start | bytes 2359304 | tf_op jit(solution)/shard_map/ppermute | solution.py:322
  68.1 42.3 %copy-start.4 = (bf16[512,768]{1,0:T(8,128)(2,1)}, bf16[512,768]{1,0:T(8,128)(2,1)S(1)}, u32[]{:S(2)}) copy-start(bf16[512,768]{1,0:T(8,128)(2,1)S(1)} %collective-permute-done.5.refs_9_) | copy-start | bytes 2359300
  68.1 52.0 %collective-permute-start.6 = (bf16[512,768]{1,0:T(8,128)(2,1)S(1)}, bf16[512,768]{1,0:T(8,128)(2,1)}, u32[]{:S(2)}, u32[]{:S(2)}) collective-permute-start(bf16[512,768]{1,0:T(8,128)(2,1)S(1)} %collective-permute-done.5.refs_9_), channel_id=1, source_target_pairs={{0,448},{4,60},{8,456},{12,4},{16,464},{20,12},{24,472},{28,20},{3... | collective-permute-start | bytes 2359304 | tf_op jit(solution)/shard_map/ppermute | solution.py:323
  82.8 23.5 %copy-start.5 = (bf16[512,1024]{1,0:T(8,128)(2,1)}, bf16[512,1024]{1,0:T(8,128)(2,1)S(1)}, u32[]{:S(2)}) copy-start(bf16[512,1024]{1,0:T(8,128)(2,1)S(1)} %collective-permute-done.10.refs_2_) | copy-start | bytes 3145732
  82.8 35.7 %collective-permute-start.7 = (bf16[256,768]{1,0:T(8,128)(2,1)}, bf16[256,768]{1,0:T(8,128)(2,1)}, u32[]{:S(2)}, u32[]{:S(2)}) collective-permute-start(bf16[256,768]{1,0:T(8,128)(2,1)} %slice.46), channel_id=1, source_target_pairs={{0,128},{4,20},{8,136},{12,28},{16,144},{20,36},{24,152},{28,44},{... | collective-permute-start | bytes 1179656 | tf_op jit(solution)/shard_map/ppermute | solution.py:325
  106.3 1.0 copy-start.6
  107.3 12.9 %collective-permute-start.8 = (bf16[256,768]{1,0:T(8,128)(2,1)}, bf16[256,768]{1,0:T(8,128)(2,1)}, u32[]{:S(2)}, u32[]{:S(2)}) collective-permute-start(bf16[256,768]{1,0:T(8,128)(2,1)} %slice.47), channel_id=1, source_target_pairs={{0,384},{4,52},{8,392},{12,60},{16,400},{20,4},{24,408},{28,12},{3... | collective-permute-start | bytes 1179656 | tf_op jit(solution)/shard_map/ppermute | solution.py:326
  120.1 0.9 copy-start.9
  121.0 30.3 %copy-start.11 = (f32[512]{0:T(512)S(1)}, f32[512]{0:T(512)}, u32[]{:S(2)}) copy-start(f32[512]{0:T(512)} %param.9) | copy-start | bytes 6148
  146.7 16.2 %all-to-all-start.2 = ((bf16[64,8,128]{2,1,0:T(8,128)(2,1)}), bf16[64,8,128]{2,1,0:T(8,128)(2,1)S(1)}, u32[]{:S(2)}, u32[]{:S(2)}) async-start(bf16[64,8,128]{2,1,0:T(8,128)(2,1)} %shard_map.58), calls=%async_computation.2 | async-start | bytes 262144 | tf_op jit(solution)/shard_map/all_to_all | solution.py:336
  163.0 0.6 copy-start.10
  166.1 9.0 %collective-permute-start.13 = (bf16[2,128,256]{2,1,0:T(8,128)(2,1)}, bf16[2,128,256]{2,1,0:T(8,128)(2,1)S(1)}, u32[]{:S(2)}, u32[]{:S(2)}) collective-permute-start(bf16[2,128,256]{2,1,0:T(8,128)(2,1)} %get-tuple-element.16), channel_id=1, source_target_pairs={{0,4},{4,0},{8,12},{12,8},{16,20},{20,16},{24,28},{28,24},{32,36},... | collective-permute-start | bytes 393224 | tf_op jit(solution)/shard_map/ppermute | solution.py:339
where the time goes:
time: 177 us; the launch traced here: 176 us
  starting transfers between devices  67.2 us (38%)
  waiting for transfers between devices  59.5 us (34%)
  Pallas kernels  20.9 us (12%)
  blocking collectives  17.9 us (10%)
  local copies, waits for them, and re-layouts  6.69 us (4%)
  other arithmetic  3.13 us (2%)
    ppermute x3, waiting for transfers between devices, body(): pieces.append(lax.ppermute(chip_tokens, 'head', ring))  30.1 us
    all_to_all x1, blocking collectives, body(): lax.all_to_all(states.reshape(chips, -1, HD), 'ctx', 0, 0, tiled=True, ax...  17.9 us
    ppermute x2, starting transfers between devices, body(): down = lax.ppermute(down, 'ctx', along_second(-1))  13.1 us
    ppermute x3, starting transfers between devices, body(): pieces.append(lax.ppermute(chip_tokens, 'head', ring))  10.5 us
    all_to_all x1, waiting for transfers between devices, body(): lax.all_to_all(copies, 'ctx', 0, 0, tiled=True, axis_index_groups=first_g...  10.1 us
    ppermute x1, starting transfers between devices, body(): came = lax.ppermute(jnp.where(is_first, high, low), 'ctx', across())  8.75 us
    all_to_all x1, waiting for transfers between devices, body(): lax.all_to_all(exclusive(slices), 'ctx', 0, 0, tiled=True, axis_index_gro...  8.43 us
    pallas_call x1, Pallas kernels, early_product(): pl.pallas_call(kernel, out_shape=(jax.ShapeDtypeStruct((rows, columns), j...  8.1 us
  transfers between devices with their start and end apart: 16, of which 8 were waited for; matrix products, arithmetic and copies ran while one was open for 2% of the time, Pallas kernels for 6%

commit v1 on v0

--- a/solution.py
+++ b/solution.py
@@ -89,12 +89,12 @@
             total[:, cols] += jnp.dot(left, right, preferred_element_type=jnp.float32)
         return 0
 
-    lax.fori_loop(0, count // 2, two, 0)
+    lax.fori_loop(0, count // 2, two, 0, unroll=True)
 
 
 def late_kernel(seqs, *refs):
-    count = len(refs) - 6
-    blocks, (left, sums, qkv, states, rhs, sems) = refs[:count], refs[count:]
+    count = len(refs) - 7
+    blocks, (left, sums, qkv, states, rhs, sems, total_ref) = refs[:count], refs[count:]
     columns = sums.shape[1]
     half, group = columns // 3, 2 * HD
     copies, ends, end = [], [], 0
@@ -109,12 +109,13 @@
     first = ends[0]
     for g in range(columns // group):
         cols = slice(g * group, (g + 1) * group)
-        sums[:, cols] += jnp.dot(left[:, :first], rhs[:first, cols], preferred_element_type=jnp.float32)
+        part = jnp.dot(left[:, :first], rhs[:first, cols], preferred_element_type=jnp.float32)
+        total_ref[:, cols] = sums[:, cols] + part
     for copy in copies[1:]:
         copy.wait()
     for g in range(columns // group):
         cols = slice(g * group, (g + 1) * group)
-        total = sums[:, cols] + jnp.dot(left[:, first:], rhs[first:, cols], preferred_element_type=jnp.float32)
+        total = total_ref[:, cols] + jnp.dot(left[:, first:], rhs[first:, cols], preferred_element_type=jnp.float32)
         if g * group < 2 * half:
             total = total / (1.0 + jnp.exp(-total))
         qkv[:, cols] = total.astype(qkv.dtype)
@@ -170,10 +171,7 @@
     rows, columns = sums.shape
 
     def kernel(*refs):
-        count = len(blocks)
-        sums_ref, total = refs[count + 1], refs[-1]
-        total[...] = sums_ref[...]
-        late_kernel(seqs, *refs[: count + 1], total, *refs[count + 2 : -1])
+        late_kernel(seqs, *refs)
 
     return pl.pallas_call(
         kernel,

time: 177 us -> 177 us (level)
  no operation moved by 1% of the time
where the time goes in v1:
time: 177 us; the launch traced here: 176 us
  starting transfers between devices  67.2 us (38%)
  waiting for transfers between devices  59 us (33%)
  Pallas kernels  21.5 us (12%)
  blocking collectives  17.9 us (10%)
  local copies, waits for them, and re-layouts  6.69 us (4%)
  other arithmetic  3.13 us (2%)
    ppermute x3, waiting for transfers between devices, body(): pieces.append(lax.ppermute(chip_tokens, 'head', ring))  30.1 us
    all_to_all x1, blocking collectives, body(): lax.all_to_all(states.reshape(chips, -1, HD), 'ctx', 0, 0, tiled=True, ax...  17.9 us
    ppermute x2, starting transfers between devices, body(): down = lax.ppermute(down, 'ctx', along_second(-1))  13.1 us
    ppermute x3, starting transfers between devices, body(): pieces.append(lax.ppermute(chip_tokens, 'head', ring))  10.5 us
    all_to_all x1, waiting for transfers between devices, body(): lax.all_to_all(copies, 'ctx', 0, 0, tiled=True, axis_index_groups=first_g...  10.1 us
    ppermute x1, starting transfers between devices, body(): came = lax.ppermute(jnp.where(is_first, high, low), 'ctx', across())  8.75 us
    pallas_call x1, Pallas kernels, early_product(): pl.pallas_call(kernel, out_shape=(jax.ShapeDtypeStruct((rows, columns), j...  8.65 us
    all_to_all x1, waiting for transfers between devices, body(): lax.all_to_all(exclusive(slices), 'ctx', 0, 0, tiled=True, axis_index_gro...  8.43 us
  transfers between devices with their start and end apart: 16, of which 8 were waited for; matrix products, arithmetic and copies ran while one was open for 2% of the time, Pallas kernels for 6%

profile of v1, /device:TPU:1, one launch (start us, length us, event | category | flops | bytes accessed | tf_op | source)
XLA Modules:
  0.0 175.8 jit_solution(9599033649859342581)
XLA Ops:
  1.6 8.7 %collective-permute-start = (bf16[32,768]{1,0:T(8,128)(2,1)S(1)}, bf16[32,768]{1,0:T(8,128)(2,1)S(1)}, u32[]{:S(2)}, u32[]{:S(2)}) collective-permute-start(bf16[32,768]{1,0:T(8,128)(2,1)S(1)} %maximum_select_fusion), channel_id=1, source_target_pairs={{0,4},{4,0},{8,12},{12,8},{16,20},{20,16},{24,28},{28,24},{32,36},... | collective-permute-start | bytes 147464 | tf_op jit(solution)/shard_map/ppermute | solution.py:296
  11.2 0.9 broadcast_in_dim.2
  12.2 3.5 %all-to-all-start = ((bf16[8,64,768]{2,1,0:T(8,128)(2,1)}), bf16[8,64,768]{2,1,0:T(8,128)(2,1)S(1)}, u32[]{:S(2)}, u32[]{:S(2)}) async-start(bf16[8,64,768]{2,1,0:T(8,128)(2,1)} %broadcast_in_dim.2), calls=%async_computation | async-start | bytes 1572864 | tf_op jit(solution)/shard_map/all_to_all | solution.py:311
  16.9 3.7 %collective-permute-start.9 = (bf16[256,1024]{1,0:T(8,128)(2,1)S(1)}, bf16[256,1024]{1,0:T(8,128)(2,1)S(1)}, u32[]{:S(2)}, u32[]{:S(2)}) collective-permute-start(bf16[256,1024]{1,0:T(8,128)(2,1)S(1)} %bitcast_select_fusion), channel_id=1, source_target_pairs={{0,4},{4,0},{8,12},{12,8},{16,20},{20,16},{24,28},{28,24},{32,36},... | collective-permute-start | bytes 1572872 | tf_op jit(solution)/shard_map/ppermute | solution.py:302
  20.6 10.1 %all-to-all-done = bf16[8,64,768]{2,1,0:T(8,128)(2,1)S(1)} async-done(((bf16[8,64,768]{2,1,0:T(8,128)(2,1)}), bf16[8,64,768]{2,1,0:T(8,128)(2,1)S(1)}, u32[]{:S(2)}, u32[]{:S(2)}) %all-to-all-start) | async-done | bytes 786464 | tf_op jit(solution)/shard_map/all_to_all | solution.py:311
  30.7 2.3 %collective-permute-start.1 = (bf16[512,768]{1,0:T(8,128)(2,1)S(1)}, bf16[512,768]{1,0:T(8,128)(2,1)S(1)}, u32[]{:S(2)}, u32[]{:S(2)}) collective-permute-start(bf16[512,768]{1,0:T(8,128)(2,1)S(1)} %bitcast.18), channel_id=1, source_target_pairs={{0,64},{4,12},{8,72},{12,20},{16,80},{20,28},{24,88},{28,36},{32,9... | collective-permute-start | bytes 2359304 | tf_op jit(solution)/shard_map/ppermute | solution.py:317
  33.0 8.3 %collective-permute-start.4 = (bf16[512,768]{1,0:T(8,128)(2,1)S(1)}, bf16[512,768]{1,0:T(8,128)(2,1)S(1)}, u32[]{:S(2)}, u32[]{:S(2)}) collective-permute-start(bf16[512,768]{1,0:T(8,128)(2,1)S(1)} %bitcast.19), channel_id=1, source_target_pairs={{0,448},{4,60},{8,456},{12,4},{16,464},{20,12},{24,472},{28,20},{3... | collective-permute-start | bytes 2359304 | tf_op jit(solution)/shard_map/ppermute | solution.py:318
  41.4 7.3 %collective-permute-done.1.refs_6_ = bf16[512,768]{1,0:T(8,128)(2,1)S(1)} collective-permute-done((bf16[512,768]{1,0:T(8,128)(2,1)S(1)}, bf16[512,768]{1,0:T(8,128)(2,1)S(1)}, u32[]{:S(2)}, u32[]{:S(2)}) %collective-permute-start.1) | collective-permute-done | bytes 786464 | tf_op jit(solution)/shard_map/ppermute | solution.py:317
  48.7 1.9 %collective-permute-start.2 = (bf16[512,768]{1,0:T(8,128)(2,1)S(1)}, bf16[512,768]{1,0:T(8,128)(2,1)S(1)}, u32[]{:S(2)}, u32[]{:S(2)}) collective-permute-start(bf16[512,768]{1,0:T(8,128)(2,1)S(1)} %collective-permute-done.1.refs_6_), channel_id=1, source_target_pairs={{0,64},{4,12},{8,72},{12,20},{16,80},{20,28},{24,88},{28,36},{32,9... | collective-permute-start | bytes 2359304 | tf_op jit(solution)/shard_map/ppermute | solution.py:317
  50.6 4.8 %collective-permute-start.5 = (bf16[512,768]{1,0:T(8,128)(2,1)S(1)}, bf16[512,768]{1,0:T(8,128)(2,1)S(1)}, u32[]{:S(2)}, u32[]{:S(2)}) collective-permute-start(bf16[512,768]{1,0:T(8,128)(2,1)S(1)} %collective-permute-done.4.refs_7_), channel_id=1, source_target_pairs={{0,448},{4,60},{8,456},{12,4},{16,464},{20,12},{24,472},{28,20},{3... | collective-permute-start | bytes 2359304 | tf_op jit(solution)/shard_map/ppermute | solution.py:318
  55.6 3.1 %collective-permute-start.10 = (bf16[512,1024]{1,0:T(8,128)(2,1)S(1)}, bf16[512,1024]{1,0:T(8,128)(2,1)S(1)}, u32[]{:S(2)}, u32[]{:S(2)}) collective-permute-start(bf16[512,1024]{1,0:T(8,128)(2,1)S(1)} %pad_maximum_fusion.refs_1_), channel_id=1, source_target_pairs={{0,1},{1,2},{2,3},{3,0},{4,5},{5,6},{6,7},{7,4},{8,9},{9,10},{10,1... | collective-permute-start | bytes 3145736 | tf_op jit(solution)/shard_map/ppermute | solution.py:307
  58.7 4.4 %collective-permute-start.11 = (bf16[512,1024]{1,0:T(8,128)(2,1)S(1)}, bf16[512,1024]{1,0:T(8,128)(2,1)S(1)}, u32[]{:S(2)}, u32[]{:S(2)}) collective-permute-start(bf16[512,1024]{1,0:T(8,128)(2,1)S(1)} %pad_maximum_fusion.refs_1_), channel_id=1, source_target_pairs={{0,2},{1,3},{2,0},{3,1},{4,6},{5,7},{6,4},{7,5},{8,10},{9,11},{10,... | collective-permute-start | bytes 3145736 | tf_op jit(solution)/shard_map/ppermute | solution.py:307
  63.1 3.1 %collective-permute-start.12 = (bf16[512,1024]{1,0:T(8,128)(2,1)S(1)}, bf16[512,1024]{1,0:T(8,128)(2,1)}, u32[]{:S(2)}, u32[]{:S(2)}) collective-permute-start(bf16[512,1024]{1,0:T(8,128)(2,1)S(1)} %pad_maximum_fusion.refs_1_), channel_id=1, source_target_pairs={{0,3},{1,0},{2,1},{3,2},{4,7},{5,4},{6,5},{7,6},{8,11},{9,8},{10,9... | collective-permute-start | bytes 3145736 | tf_op jit(solution)/shard_map/ppermute | solution.py:307
  66.2 1.9 %collective-permute-start.3 = (bf16[512,768]{1,0:T(8,128)(2,1)S(1)}, bf16[512,768]{1,0:T(8,128)(2,1)S(1)}, u32[]{:S(2)}, u32[]{:S(2)}) collective-permute-start(bf16[512,768]{1,0:T(8,128)(2,1)S(1)} %collective-permute-done.2.refs_8_), channel_id=1, source_target_pairs={{0,64},{4,12},{8,72},{12,20},{16,80},{20,28},{24,88},{28,36},{32,9... | collective-permute-start | bytes 2359304 | tf_op jit(solution)/shard_map/ppermute | solution.py:320
  68.1 4.6 %collective-permute-start.6 = (bf16[512,768]{1,0:T(8,128)(2,1)S(1)}, bf16[512,768]{1,0:T(8,128)(2,1)}, u32[]{:S(2)}, u32[]{:S(2)}) collective-permute-start(bf16[512,768]{1,0:T(8,128)(2,1)S(1)} %collective-permute-done.5.refs_9_), channel_id=1, source_target_pairs={{0,448},{4,60},{8,456},{12,4},{16,464},{20,12},{24,472},{28,20},{3... | collective-permute-start | bytes 2359304 | tf_op jit(solution)/shard_map/ppermute | solution.py:321
  74.3 8.6 %collective-permute-done.10.refs_2_ = bf16[512,1024]{1,0:T(8,128)(2,1)S(1)} collective-permute-done((bf16[512,1024]{1,0:T(8,128)(2,1)S(1)}, bf16[512,1024]{1,0:T(8,128)(2,1)S(1)}, u32[]{:S(2)}, u32[]{:S(2)}) %collective-permute-start.10) | collective-permute-done | bytes 1048608 | tf_op jit(solution)/shard_map/ppermute | solution.py:307
  82.8 1.9 %collective-permute-start.7 = (bf16[256,768]{1,0:T(8,128)(2,1)}, bf16[256,768]{1,0:T(8,128)(2,1)}, u32[]{:S(2)}, u32[]{:S(2)}) collective-permute-start(bf16[256,768]{1,0:T(8,128)(2,1)} %slice.46), channel_id=1, source_target_pairs={{0,128},{4,20},{8,136},{12,28},{16,144},{20,36},{24,152},{28,44},{... | collective-permute-start | bytes 1179656 | tf_op jit(solution)/shard_map/ppermute | solution.py:323
  84.8 21.5 %collective-permute-done.11.refs_3_ = bf16[512,1024]{1,0:T(8,128)(2,1)S(1)} collective-permute-done((bf16[512,1024]{1,0:T(8,128)(2,1)S(1)}, bf16[512,1024]{1,0:T(8,128)(2,1)S(1)}, u32[]{:S(2)}, u32[]{:S(2)}) %collective-permute-start.11) | collective-permute-done | bytes 1048608 | tf_op jit(solution)/shard_map/ppermute | solution.py:307
  106.3 1.0 copy-done.6
  107.3 2.5 %collective-permute-start.8 = (bf16[256,768]{1,0:T(8,128)(2,1)}, bf16[256,768]{1,0:T(8,128)(2,1)}, u32[]{:S(2)}, u32[]{:S(2)}) collective-permute-start(bf16[256,768]{1,0:T(8,128)(2,1)} %slice.47), channel_id=1, source_target_pairs={{0,384},{4,52},{8,392},{12,60},{16,400},{20,4},{24,408},{28,12},{3... | collective-permute-start | bytes 1179656 | tf_op jit(solution)/shard_map/ppermute | solution.py:324
  110.5 8.7 %shard_map.55 = (f32[512,768]{1,0:T(8,128)}, bf16[512,1536]{1,0:T(8,128)(2,1)}) custom-call(s32[3]{0:T(128)} %pad_add_fusion.refs_0_, bf16[512,1024]{1,0:T(8,128)(2,1)} %copy-done.1, bf16[512,1024]{1,0:T(8,128)(2,1)} %copy-done.5, bf16[512,1024]{1,0:T(8,128)(2,1)} %copy-done.6, bf16[512,1024]{1,0:T(8,128)(2,1)} %collective-permute-done.12.refs_4_, ...), custom_call_target="tpu_custom_call" | custom-call | flops 2013265920 | bytes 8388608 | tf_op jit(solution)/shard_map/pallas_call | solution.py:150
  119.1 1.0 collective-permute-done.8.refs_3_
  120.2 0.9 copy-done.9
  121.0 6.2 %shard_map.56 = (bf16[512,768]{1,0:T(8,128)(2,1)}, f32[2,2,128,128]{3,2,1,0:T(8,128)}) custom-call(bf16[512,768]{1,0:T(8,128)(2,1)} %copy-done.9, bf16[512,768]{1,0:T(8,128)(2,1)} %collective-permute-done.6.refs_1_, bf16[256,768]{1,0:T(8,128)(2,1)} %collective-permute-done.7.refs_2_, bf16[256,768]{1,0:T(8,128)(2,1)} %collective-permute-done.8.refs_3_, ...), custom_call_target="tpu_custom_call" | custom-call | tf_op jit(solution)/shard_map/pallas_call | solution.py:176
  127.2 17.9 %all_to_all.15.slices_ref = f32[64,8,128]{2,1,0:T(8,128)} all-to-all(f32[64,8,128]{2,1,0:T(8,128)} %bitcast.24), channel_id=1, replica_groups={{0,8,16,24,32,40,48,56,64,72,80,88,96,104,112,120,128,136,144,152,160,1..., dimensions={0} | all-to-all | bytes 524288 | tf_op jit(solution)/shard_map/all_to_all | solution.py:330
  145.1 1.7 shard_map.58
  146.8 4.6 %all-to-all-start.2 = ((bf16[64,8,128]{2,1,0:T(8,128)(2,1)}), bf16[64,8,128]{2,1,0:T(8,128)(2,1)S(1)}, u32[]{:S(2)}, u32[]{:S(2)}) async-start(bf16[64,8,128]{2,1,0:T(8,128)(2,1)} %shard_map.58), calls=%async_computation.2 | async-start | bytes 262144 | tf_op jit(solution)/shard_map/all_to_all | solution.py:334
  152.0 2.6 %shard_map.57.refs_2_ = f32[2,2,256,128]{3,2,1,0:T(8,128)} custom-call(bf16[512,768]{1,0:T(8,128)(2,1)} %get-tuple-element.13.refs_0_.refs_1_), custom_call_target="tpu_custom_call" | custom-call | tf_op jit(solution)/shard_map/pallas_call | solution.py:234
  154.6 8.4 %all-to-all-done.2 = bf16[64,8,128]{2,1,0:T(8,128)(2,1)S(1)} async-done(((bf16[64,8,128]{2,1,0:T(8,128)(2,1)}), bf16[64,8,128]{2,1,0:T(8,128)(2,1)S(1)}, u32[]{:S(2)}, u32[]{:S(2)}) %all-to-all-start.2) | async-done | bytes 131104 | tf_op jit(solution)/shard_map/all_to_all | solution.py:334
  163.7 2.4 %shard_map.59 = (bf16[2,128,512]{2,1,0:T(8,128)(2,1)}, bf16[2,128,256]{2,1,0:T(8,128)(2,1)}) custom-call(s32[3]{0:T(128)} %pad_add_fusion.refs_0_, bf16[512,768]{1,0:T(8,128)(2,1)} %get-tuple-element.13.refs_0_.refs_1_, f32[2,2,256,128]{3,2,1,0:T(8,128)} %shard_map.57.refs_2_, bf16[2,2,128,128]{3,2,1,0:T(8,128)(2,1)} %bitcast.23, f32[1,256]{1,0:T(1,128)} %bitcast.25), custom_call_target="tpu_custom_call" | custom-call | tf_op jit(solution)/shard_map/pallas_call | solution.py:264
  166.1 7.9 %collective-permute-start.13 = (bf16[2,128,256]{2,1,0:T(8,128)(2,1)}, bf16[2,128,256]{2,1,0:T(8,128)(2,1)S(1)}, u32[]{:S(2)}, u32[]{:S(2)}) collective-permute-start(bf16[2,128,256]{2,1,0:T(8,128)(2,1)} %get-tuple-element.16), channel_id=1, source_target_pairs={{0,4},{4,0},{8,12},{12,8},{16,20},{20,16},{24,28},{28,24},{32,36},... | collective-permute-start | bytes 393224 | tf_op jit(solution)/shard_map/ppermute | solution.py:337
  174.0 1.2 collective-permute-done.13
  (48 shorter events, 7.9 us)
Async XLA Ops:
  0.7 15.0 %copy-start = (bf16[2,128,1024]{2,1,0:T(8,128)(2,1)S(1)}, bf16[2,128,1024]{2,1,0:T(8,128)(2,1)}, u32[]{:S(2)}) copy-start(bf16[2,128,1024]{2,1,0:T(8,128)(2,1)} %param.5) | copy-start | bytes 1572868
  1.6 9.6 %collective-permute-start = (bf16[32,768]{1,0:T(8,128)(2,1)S(1)}, bf16[32,768]{1,0:T(8,128)(2,1)S(1)}, u32[]{:S(2)}, u32[]{:S(2)}) collective-permute-start(bf16[32,768]{1,0:T(8,128)(2,1)S(1)} %maximum_select_fusion), channel_id=1, source_target_pairs={{0,4},{4,0},{8,12},{12,8},{16,20},{20,16},{24,28},{28,24},{32,36},... | collective-permute-start | bytes 147464 | tf_op jit(solution)/shard_map/ppermute | solution.py:296
  12.2 18.5 %all-to-all-start = ((bf16[8,64,768]{2,1,0:T(8,128)(2,1)}), bf16[8,64,768]{2,1,0:T(8,128)(2,1)S(1)}, u32[]{:S(2)}, u32[]{:S(2)}) async-start(bf16[8,64,768]{2,1,0:T(8,128)(2,1)} %broadcast_in_dim.2), calls=%async_computation | async-start | bytes 1572864 | tf_op jit(solution)/shard_map/all_to_all | solution.py:311
  16.9 24.4 %collective-permute-start.9 = (bf16[256,1024]{1,0:T(8,128)(2,1)S(1)}, bf16[256,1024]{1,0:T(8,128)(2,1)S(1)}, u32[]{:S(2)}, u32[]{:S(2)}) collective-permute-start(bf16[256,1024]{1,0:T(8,128)(2,1)S(1)} %bitcast_select_fusion), channel_id=1, source_target_pairs={{0,4},{4,0},{8,12},{12,8},{16,20},{20,16},{24,28},{28,24},{32,36},... | collective-permute-start | bytes 1572872 | tf_op jit(solution)/shard_map/ppermute | solution.py:302
  30.7 24.9 %copy-start.2 = (bf16[8,64,768]{2,1,0:T(8,128)(2,1)}, bf16[8,64,768]{2,1,0:T(8,128)(2,1)S(1)}, u32[]{:S(2)}) copy-start(bf16[8,64,768]{2,1,0:T(8,128)(2,1)S(1)} %all-to-all-done) | copy-start | bytes 2359300
  30.7 18.0 %collective-permute-start.1 = (bf16[512,768]{1,0:T(8,128)(2,1)S(1)}, bf16[512,768]{1,0:T(8,128)(2,1)S(1)}, u32[]{:S(2)}, u32[]{:S(2)}) collective-permute-start(bf16[512,768]{1,0:T(8,128)(2,1)S(1)} %bitcast.18), channel_id=1, source_target_pairs={{0,64},{4,12},{8,72},{12,20},{16,80},{20,28},{24,88},{28,36},{32,9... | collective-permute-start | bytes 2359304 | tf_op jit(solution)/shard_map/ppermute | solution.py:317
  33.0 17.7 %collective-permute-start.4 = (bf16[512,768]{1,0:T(8,128)(2,1)S(1)}, bf16[512,768]{1,0:T(8,128)(2,1)S(1)}, u32[]{:S(2)}, u32[]{:S(2)}) collective-permute-start(bf16[512,768]{1,0:T(8,128)(2,1)S(1)} %bitcast.19), channel_id=1, source_target_pairs={{0,448},{4,60},{8,456},{12,4},{16,464},{20,12},{24,472},{28,20},{3... | collective-permute-start | bytes 2359304 | tf_op jit(solution)/shard_map/ppermute | solution.py:318
  48.7 25.6 %copy-start.7 = (bf16[512,768]{1,0:T(8,128)(2,1)}, bf16[512,768]{1,0:T(8,128)(2,1)S(1)}, u32[]{:S(2)}) copy-start(bf16[512,768]{1,0:T(8,128)(2,1)S(1)} %collective-permute-done.1.refs_6_) | copy-start | bytes 2359300
  48.7 17.5 %collective-permute-start.2 = (bf16[512,768]{1,0:T(8,128)(2,1)S(1)}, bf16[512,768]{1,0:T(8,128)(2,1)S(1)}, u32[]{:S(2)}, u32[]{:S(2)}) collective-permute-start(bf16[512,768]{1,0:T(8,128)(2,1)S(1)} %collective-permute-done.1.refs_6_), channel_id=1, source_target_pairs={{0,64},{4,12},{8,72},{12,20},{16,80},{20,28},{24,88},{28,36},{32,9... | collective-permute-start | bytes 2359304 | tf_op jit(solution)/shard_map/ppermute | solution.py:317
  50.6 23.6 %copy-start.8 = (bf16[512,768]{1,0:T(8,128)(2,1)}, bf16[512,768]{1,0:T(8,128)(2,1)S(1)}, u32[]{:S(2)}) copy-start(bf16[512,768]{1,0:T(8,128)(2,1)S(1)} %collective-permute-done.4.refs_7_) | copy-start | bytes 2359300
  50.6 17.5 %collective-permute-start.5 = (bf16[512,768]{1,0:T(8,128)(2,1)S(1)}, bf16[512,768]{1,0:T(8,128)(2,1)S(1)}, u32[]{:S(2)}, u32[]{:S(2)}) collective-permute-start(bf16[512,768]{1,0:T(8,128)(2,1)S(1)} %collective-permute-done.4.refs_7_), channel_id=1, source_target_pairs={{0,448},{4,60},{8,456},{12,4},{16,464},{20,12},{24,472},{28,20},{3... | collective-permute-start | bytes 2359304 | tf_op jit(solution)/shard_map/ppermute | solution.py:318
  55.6 54.9 %copy-start.1 = (bf16[512,1024]{1,0:T(8,128)(2,1)}, bf16[512,1024]{1,0:T(8,128)(2,1)S(1)}, u32[]{:S(2)}) copy-start(bf16[512,1024]{1,0:T(8,128)(2,1)S(1)} %pad_maximum_fusion.refs_1_) | copy-start | bytes 3145732
  55.6 27.2 %collective-permute-start.10 = (bf16[512,1024]{1,0:T(8,128)(2,1)S(1)}, bf16[512,1024]{1,0:T(8,128)(2,1)S(1)}, u32[]{:S(2)}, u32[]{:S(2)}) collective-permute-start(bf16[512,1024]{1,0:T(8,128)(2,1)S(1)} %pad_maximum_fusion.refs_1_), channel_id=1, source_target_pairs={{0,1},{1,2},{2,3},{3,0},{4,5},{5,6},{6,7},{7,4},{8,9},{9,10},{10,1... | collective-permute-start | bytes 3145736 | tf_op jit(solution)/shard_map/ppermute | solution.py:307
  58.7 47.6 %collective-permute-start.11 = (bf16[512,1024]{1,0:T(8,128)(2,1)S(1)}, bf16[512,1024]{1,0:T(8,128)(2,1)S(1)}, u32[]{:S(2)}, u32[]{:S(2)}) collective-permute-start(bf16[512,1024]{1,0:T(8,128)(2,1)S(1)} %pad_maximum_fusion.refs_1_), channel_id=1, source_target_pairs={{0,2},{1,3},{2,0},{3,1},{4,6},{5,7},{6,4},{7,5},{8,10},{9,11},{10,... | collective-permute-start | bytes 3145736 | tf_op jit(solution)/shard_map/ppermute | solution.py:307
  63.1 47.4 %collective-permute-start.12 = (bf16[512,1024]{1,0:T(8,128)(2,1)S(1)}, bf16[512,1024]{1,0:T(8,128)(2,1)}, u32[]{:S(2)}, u32[]{:S(2)}) collective-permute-start(bf16[512,1024]{1,0:T(8,128)(2,1)S(1)} %pad_maximum_fusion.refs_1_), channel_id=1, source_target_pairs={{0,3},{1,0},{2,1},{3,2},{4,7},{5,4},{6,5},{7,6},{8,11},{9,8},{10,9... | collective-permute-start | bytes 3145736 | tf_op jit(solution)/shard_map/ppermute | solution.py:307
  66.2 44.3 %copy-start.3 = (bf16[512,768]{1,0:T(8,128)(2,1)}, bf16[512,768]{1,0:T(8,128)(2,1)S(1)}, u32[]{:S(2)}) copy-start(bf16[512,768]{1,0:T(8,128)(2,1)S(1)} %collective-permute-done.2.refs_8_) | copy-start | bytes 2359300
  66.2 54.0 %collective-permute-start.3 = (bf16[512,768]{1,0:T(8,128)(2,1)S(1)}, bf16[512,768]{1,0:T(8,128)(2,1)S(1)}, u32[]{:S(2)}, u32[]{:S(2)}) collective-permute-start(bf16[512,768]{1,0:T(8,128)(2,1)S(1)} %collective-permute-done.2.refs_8_), channel_id=1, source_target_pairs={{0,64},{4,12},{8,72},{12,20},{16,80},{20,28},{24,88},{28,36},{32,9... | collective-permute-start | bytes 2359304 | tf_op jit(solution)/shard_map/ppermute | solution.py:320
  68.1 42.3 %copy-start.4 = (bf16[512,768]{1,0:T(8,128)(2,1)}, bf16[512,768]{1,0:T(8,128)(2,1)S(1)}, u32[]{:S(2)}) copy-start(bf16[512,768]{1,0:T(8,128)(2,1)S(1)} %collective-permute-done.5.refs_9_) | copy-start | bytes 2359300
  68.1 52.0 %collective-permute-start.6 = (bf16[512,768]{1,0:T(8,128)(2,1)S(1)}, bf16[512,768]{1,0:T(8,128)(2,1)}, u32[]{:S(2)}, u32[]{:S(2)}) collective-permute-start(bf16[512,768]{1,0:T(8,128)(2,1)S(1)} %collective-permute-done.5.refs_9_), channel_id=1, source_target_pairs={{0,448},{4,60},{8,456},{12,4},{16,464},{20,12},{24,472},{28,20},{3... | collective-permute-start | bytes 2359304 | tf_op jit(solution)/shard_map/ppermute | solution.py:321
  82.8 23.5 %copy-start.5 = (bf16[512,1024]{1,0:T(8,128)(2,1)}, bf16[512,1024]{1,0:T(8,128)(2,1)S(1)}, u32[]{:S(2)}) copy-start(bf16[512,1024]{1,0:T(8,128)(2,1)S(1)} %collective-permute-done.10.refs_2_) | copy-start | bytes 3145732
  82.8 36.3 %collective-permute-start.7 = (bf16[256,768]{1,0:T(8,128)(2,1)}, bf16[256,768]{1,0:T(8,128)(2,1)}, u32[]{:S(2)}, u32[]{:S(2)}) collective-permute-start(bf16[256,768]{1,0:T(8,128)(2,1)} %slice.46), channel_id=1, source_target_pairs={{0,128},{4,20},{8,136},{12,28},{16,144},{20,36},{24,152},{28,44},{... | collective-permute-start | bytes 1179656 | tf_op jit(solution)/shard_map/ppermute | solution.py:323
  106.3 1.0 copy-start.6
  107.3 12.9 %collective-permute-start.8 = (bf16[256,768]{1,0:T(8,128)(2,1)}, bf16[256,768]{1,0:T(8,128)(2,1)}, u32[]{:S(2)}, u32[]{:S(2)}) collective-permute-start(bf16[256,768]{1,0:T(8,128)(2,1)} %slice.47), channel_id=1, source_target_pairs={{0,384},{4,52},{8,392},{12,60},{16,400},{20,4},{24,408},{28,12},{3... | collective-permute-start | bytes 1179656 | tf_op jit(solution)/shard_map/ppermute | solution.py:324
  120.1 0.9 copy-start.9
  121.0 30.4 %copy-start.11 = (f32[512]{0:T(512)S(1)}, f32[512]{0:T(512)}, u32[]{:S(2)}) copy-start(f32[512]{0:T(512)} %param.9) | copy-start | bytes 6148
  146.8 16.2 %all-to-all-start.2 = ((bf16[64,8,128]{2,1,0:T(8,128)(2,1)}), bf16[64,8,128]{2,1,0:T(8,128)(2,1)S(1)}, u32[]{:S(2)}, u32[]{:S(2)}) async-start(bf16[64,8,128]{2,1,0:T(8,128)(2,1)} %shard_map.58), calls=%async_computation.2 | async-start | bytes 262144 | tf_op jit(solution)/shard_map/all_to_all | solution.py:334
  163.1 0.6 copy-start.10
  166.1 9.0 %collective-permute-start.13 = (bf16[2,128,256]{2,1,0:T(8,128)(2,1)}, bf16[2,128,256]{2,1,0:T(8,128)(2,1)S(1)}, u32[]{:S(2)}, u32[]{:S(2)}) collective-permute-start(bf16[2,128,256]{2,1,0:T(8,128)(2,1)} %get-tuple-element.16), channel_id=1, source_target_pairs={{0,4},{4,0},{8,12},{12,8},{16,20},{20,16},{24,28},{28,24},{32,36},... | collective-permute-start | bytes 393224 | tf_op jit(solution)/shard_map/ppermute | solution.py:337
